TPU v7x, 32 devices: a whole 2x2x4 slice. The times are simulated.
32 devices in a mesh: batch: 8 (over z, x), rows: 4 (over y, core).
Axes of the slice: x: 2, y: 2, z: 4, core: 2. Of those that a mesh axis runs over, the one named last changes fastest.
Arguments:
- pixels: int32 [12, 16, 16, 1024], P(None, 'rows', None, 'batch'), may hold values from 0 to 255
- valid_mask: int32 [16, 16, 1024], P('rows', None, 'batch'), may hold values from 0 to 1, as said below
- vectors: float32 [2960], replicated, may hold values from -0.8 to 0.8
- vectors_first: float32 [2960], replicated, may hold values from -7.6293945e-06 to 7.6293945e-06
- vectors_second: float32 [2960], replicated, may hold values from 6.357699e-14 to 5.0861594e-13
- entry_taps: float32 [9, 18, 512], replicated, may hold values from -0.625 to 0.625
- entry_first: float32 [9, 18, 512], replicated, may hold values from -1.4305115e-06 to 1.4305115e-06
- entry_second: float32 [9, 18, 512], replicated, may hold values from 3.1788496e-15 to 2.5430797e-14
- middle: float32 [2, 512, 512], replicated, may hold values from -0.25 to 0.25
- middle_first: float32 [2, 512, 512], replicated, may hold values from -7.6293945e-06 to 7.6293945e-06
- middle_second: float32 [2, 512, 512], replicated, may hold values from 6.357699e-14 to 5.0861594e-13
- exit_taps: float32 [9, 36, 512], replicated, may hold values from -0.046875 to 0.046875
- exit_first: float32 [9, 36, 512], replicated, may hold values from -7.6293945e-06 to 7.6293945e-06
- exit_second: float32 [9, 36, 512], replicated, may hold values from 6.357699e-14 to 5.0861594e-13
- prior_taps: float32 [9, 48, 24], replicated, may hold values from -0.21875 to 0.21875
- prior_first: float32 [9, 48, 24], replicated, may hold values from -7.6293945e-06 to 7.6293945e-06
- prior_second: float32 [9, 48, 24], replicated, may hold values from 6.357699e-14 to 5.0861594e-13
Outputs:
- loss: float32 [], replicated
- grad_norm: float32 [], replicated
- vectors_new: float32 [2960], replicated
- vectors_grad: float32 [2960], replicated
- vectors_moment: float32 [2960], replicated
- entry_new: float32 [9, 18, 512], replicated
- entry_grad: float32 [9, 18, 512], replicated
- entry_moment: float32 [9, 18, 512], replicated
- middle_new: float32 [2, 512, 512], replicated
- middle_grad: float32 [2, 512, 512], replicated
- middle_moment: float32 [2, 512, 512], replicated
- exit_new: float32 [9, 36, 512], replicated
- exit_grad: float32 [9, 36, 512], replicated
- exit_moment: float32 [9, 36, 512], replicated
- prior_new: float32 [9, 48, 24], replicated
- prior_grad: float32 [9, 48, 24], replicated
- prior_moment: float32 [9, 48, 24], replicated
- bias_grads: float32 [4, 512], replicated
Inputs may be any that keep to these rules, and one draw needn't show every extreme that they name: `valid_mask`: 0 or 1; the first pixel (row 0, column 0) of every image is 1.
All inputs are finite; a program needn't handle non-finite values.
Results may differ from a plain program's by a relative error of at most 0.0055.
The roundings to bfloat16 on the way count: a program that leaves them out, or rounds other values in their place, can miss the bound.
Values may be sent and summed in bfloat16 or wider, within the bound.
No kernel may reach another device: no remote copies, remote signals or barrier semaphores. Data moves between devices by JAX's collectives and lax.ppermute only.
A program may use at most 448 MiB of HBM per device.

v0:
```python
import math
import jax
import jax.numpy as jnp
from jax import lax
from jax.sharding import PartitionSpec as P

HID = 512
CH = 12
HIGH = lax.Precision.HIGHEST
LOG_TWO_PI = math.log(2.0 * math.pi)
LEARN_RATE = 0.05
BETA_ONE = 0.9
BETA_TWO = 0.999
ADAM_EPS = 1e-08
WEIGHT_DECAY = 0.01
CLIP_NORM = 0.01
ADAM_STEP = 10


def padded_2(shard, sides, width):
    for axis, dim in sides:
        size, length = (lax.axis_size(axis), shard.shape[dim])
        up = [(i, (i + 1) % size) for i in range(size - 1)]
        down = [(j, i) for i, j in up]
        last = lax.slice_in_dim(shard, length - width, length, axis=dim)
        first = lax.slice_in_dim(shard, 0, width, axis=dim)
        before = lax.ppermute(last, axis, up)
        after = lax.ppermute(first, axis, down)
        shard = jnp.concatenate([before, shard, after], axis=dim)
    return shard


def conv_taps(source, weight):
    row_count = source.shape[1] - 2
    col_count = source.shape[2]
    padded = jnp.pad(source, ((0, 0), (0, 0), (1, 1), (0, 0)))
    total = None
    for tap_index in range(9):
        shift_row, shift_col = (tap_index // 3, tap_index % 3)
        window = padded[:, shift_row : shift_row + row_count, shift_col : shift_col + col_count, :]
        term = lax.dot_general(
            weight[tap_index], window, (((1,), (0,)), ((), ())), preferred_element_type=jnp.float32
        )
        total = term if total is None else total + term
    return total


def tap_grads(source, grad):
    row_count, col_count = (grad.shape[1], grad.shape[2])
    padded = jnp.pad(source, ((0, 0), (0, 0), (1, 1), (0, 0)))
    pieces = []
    for tap_index in range(9):
        shift_row, shift_col = (tap_index // 3, tap_index % 3)
        window = padded[:, shift_row : shift_row + row_count, shift_col : shift_col + col_count, :]
        pieces.append(
            lax.dot_general(
                grad, window, (((1, 2, 3), (1, 2, 3)), ((), ())), preferred_element_type=jnp.float32
            )
        )
    return jnp.stack(pieces)


def turn_taps(weight):
    return jnp.swapaxes(weight[::-1], 1, 2)


def stretch(field):
    return padded_2(field, (("rows", 1),), 2)


def stretch_back(field):
    return padded_2(field, (("rows", 1),), 2)


def edge_rows(row_count):
    first_row = lax.axis_index("rows") * row_count
    total_rows = row_count * lax.axis_size("rows")
    placed = first_row + jnp.arange(row_count + 2) - 1
    return ((placed >= 0) & (placed < total_rows)).astype(jnp.float32)


def level_params(vectors, entry_taps, middle, exit_taps, level_index):
    chans = CH * (level_index + 1)
    half_size = chans // 2
    offset = 0 if level_index == 0 else 4 * CH + 2 * HID + CH * CH
    segment = vectors[offset : offset + 4 * chans + 2 * HID + chans * chans]
    first_in = 0 if level_index == 0 else CH // 2
    first_out = 0 if level_index == 0 else CH
    return {
        "chan": segment[: 4 * chans].reshape(4, chans),
        "bias_a": segment[4 * chans : 4 * chans + HID],
        "bias_b": segment[4 * chans + HID : 4 * chans + 2 * HID],
        "lu_mix": segment[4 * chans + 2 * HID :].reshape(chans, chans),
        "weight_a": jnp.swapaxes(entry_taps[:, first_in : first_in + half_size], 1, 2).astype(
            jnp.bfloat16
        ),
        "weight_b": middle[level_index].astype(jnp.bfloat16),
        "weight_c": exit_taps[:, first_out : first_out + chans].astype(jnp.bfloat16),
    }


def hidden_biases(vector_grad):
    second_start = 4 * CH + 2 * HID + CH * CH
    first_part = vector_grad[4 * CH : 4 * CH + 2 * HID]
    second_part = vector_grad[second_start + 8 * CH : second_start + 8 * CH + 2 * HID]
    return jnp.concatenate([first_part, second_part]).reshape(4, HID)


def mix_channels(source, chan, lu_mix):
    chans = lu_mix.shape[0]
    shifted = (source + chan[0][:, None, None, None]) * jnp.exp(chan[1])[:, None, None, None]
    lower = jnp.tril(lu_mix, -1) + jnp.eye(chans, dtype=jnp.float32)
    upper = jnp.triu(lu_mix, 1) + jnp.diag(jnp.exp(chan[2]))
    matrix = jnp.dot(lower, upper, precision=HIGH)[::-1]
    mixed = jnp.tensordot(matrix, shifted, axes=1, precision=HIGH)
    return (mixed, jnp.sum(chan[1]) + jnp.sum(chan[2]))


def affine_head(second_half, output):
    half_size = second_half.shape[0]
    scale_log = jax.nn.log_sigmoid(output[half_size:] + 2.0)
    result = (second_half + output[:half_size]) * jnp.exp(scale_log)
    return (result, jnp.sum(scale_log, axis=0))


def gauss_log(dropped, prior):
    half_size = dropped.shape[0]
    mean_part, log_part = (prior[:half_size], prior[half_size:])
    scaled = (dropped - mean_part) * jnp.exp(-log_part)
    return jnp.sum(-0.5 * LOG_TWO_PI - log_part - 0.5 * scaled * scaled, axis=0)


def squeeze(field):
    chans, row_count, col_count = (field.shape[0], field.shape[1], field.shape[2])
    rest = field.shape[3:]
    parted = field.reshape((chans, row_count // 2, 2, col_count // 2, 2) + rest)
    moved = jnp.moveaxis(parted, (2, 4), (1, 2))
    return moved.reshape((chans * 4, row_count // 2, col_count // 2) + rest)


def unsqueeze(field):
    chans = field.shape[0] // 4
    parted = field.reshape((chans, 2, 2) + field.shape[1:])
    moved = jnp.moveaxis(parted, (1, 2), (2, 4))
    return moved.reshape((chans, field.shape[1] * 2, field.shape[2] * 2) + field.shape[3:])


def couple_forward(mixed, params):
    half_size = mixed.shape[0] // 2
    row_count = mixed.shape[1]
    inner_ext = stretch(mixed[:half_size].astype(jnp.bfloat16))
    pre_one = conv_taps(inner_ext, params["weight_a"]) + params["bias_a"][:, None, None, None]
    hidden_one = jnp.maximum(pre_one, 0.0).astype(jnp.bfloat16)
    pre_two = (
        lax.dot_general(
            params["weight_b"],
            hidden_one,
            (((1,), (0,)), ((), ())),
            preferred_element_type=jnp.float32,
        )
        + params["bias_b"][:, None, None, None]
    )
    inside = edge_rows(row_count)[None, :, None, None]
    hidden_two = (jnp.maximum(pre_two, 0.0) * inside).astype(jnp.bfloat16)
    output = conv_taps(hidden_two, params["weight_c"]) + params["chan"][3][:, None, None, None]
    (result, step_log), head_back = jax.vjp(affine_head, mixed[half_size:], output)
    return (
        jnp.concatenate([mixed[:half_size], result]),
        step_log,
        (inner_ext, hidden_one, hidden_two, head_back),
    )


def couple_backward(grad_out, grad_log, saved, params):
    inner_ext, hidden_one, hidden_two, head_back = saved
    half_size = grad_out.shape[0] // 2
    row_count = grad_out.shape[1]
    grad_second, grad_output = head_back((grad_out[half_size:], grad_log))
    output_low = grad_output.astype(jnp.bfloat16)
    bias_c = jnp.sum(output_low.astype(jnp.float32), axis=(1, 2, 3))
    taps_c = tap_grads(hidden_two, output_low)
    output_ext = stretch_back(output_low)
    grad_hidden_two = conv_taps(output_ext, turn_taps(params["weight_c"]))
    pre_two_low = jnp.where(hidden_two > 0, grad_hidden_two, 0.0).astype(jnp.bfloat16)
    own_two = pre_two_low[:, 1 : row_count + 1]
    bias_b = jnp.sum(own_two.astype(jnp.float32), axis=(1, 2, 3))
    weight_b = lax.dot_general(
        own_two,
        hidden_one[:, 1 : row_count + 1],
        (((1, 2, 3), (1, 2, 3)), ((), ())),
        preferred_element_type=jnp.float32,
    )
    grad_hidden_one = lax.dot_general(
        params["weight_b"],
        pre_two_low,
        (((0,), (0,)), ((), ())),
        preferred_element_type=jnp.float32,
    )
    pre_one_low = jnp.where(hidden_one > 0, grad_hidden_one, 0.0).astype(jnp.bfloat16)
    own_one = pre_one_low[:, 1 : row_count + 1]
    bias_a = jnp.sum(own_one.astype(jnp.float32), axis=(1, 2, 3))
    taps_a = jnp.swapaxes(tap_grads(inner_ext[:, 1 : row_count + 3], own_one), 1, 2)
    grad_first = grad_out[:half_size] + conv_taps(pre_one_low, turn_taps(params["weight_a"]))
    grads = {
        "bias_a": bias_a,
        "bias_b": bias_b,
        "bias_c": bias_c,
        "taps_a": taps_a,
        "weight_b": weight_b,
        "taps_c": taps_c,
    }
    return (jnp.concatenate([grad_first, grad_second]), grads)


def pack_level(chan_grad, lu_grad, grads):
    chan_full = chan_grad.at[3].add(grads["bias_c"])
    return jnp.concatenate(
        [chan_full.reshape(-1), grads["bias_a"], grads["bias_b"], lu_grad.reshape(-1)]
    )


def adamw(weight, grad, first, second):
    first_new = BETA_ONE * first + (1.0 - BETA_ONE) * grad
    second_new = BETA_TWO * second + (1.0 - BETA_TWO) * grad * grad
    first_hat = first_new / (1.0 - BETA_ONE**ADAM_STEP)
    second_hat = second_new / (1.0 - BETA_TWO**ADAM_STEP)
    updated = weight - LEARN_RATE * (
        first_hat / (jnp.sqrt(second_hat) + ADAM_EPS) + WEIGHT_DECAY * weight
    )
    return (updated, second_new)


def on_device(
    pixels,
    valid_mask,
    vectors,
    vectors_first,
    vectors_second,
    entry_taps,
    entry_first,
    entry_second,
    middle,
    middle_first,
    middle_second,
    exit_taps,
    exit_first,
    exit_second,
    prior_taps,
    prior_first,
    prior_second,
):
    source = (pixels.astype(jnp.float32) + 0.5) / 256.0 - 0.5
    mask_one = valid_mask.astype(jnp.float32)
    first_params = level_params(vectors, entry_taps, middle, exit_taps, 0)
    second_params = level_params(vectors, entry_taps, middle, exit_taps, 1)
    prior_low_taps = prior_taps.astype(jnp.bfloat16)
    (mixed_one, const_one), mix_back_one = jax.vjp(
        mix_channels, source, first_params["chan"], first_params["lu_mix"]
    )
    out_one, step_one, saved_one = couple_forward(mixed_one, first_params)
    folded = squeeze(out_one)
    keep_part, drop_part = (folded[: 2 * CH], folded[2 * CH :])
    row_count, col_count = (mask_one.shape[0], mask_one.shape[1])
    mask_two = jnp.min(mask_one.reshape(row_count // 2, 2, col_count // 2, 2, -1), axis=(1, 3))
    keep_ext = stretch(keep_part.astype(jnp.bfloat16))[:, 1:-1]
    prior = conv_taps(keep_ext, prior_low_taps) + vectors[-4 * CH :][:, None, None, None]
    drop_log, prior_back = jax.vjp(gauss_log, drop_part, prior)
    level_input, level_mask = (keep_part, mask_two)
    (mixed_two, const_two), mix_back_two = jax.vjp(
        mix_channels, level_input, second_params["chan"], second_params["lu_mix"]
    )
    out_two, step_two, saved_two = couple_forward(mixed_two, second_params)
    top_log = jnp.sum(-0.5 * (LOG_TWO_PI + out_two * out_two), axis=0)
    local_total = (
        jnp.sum(mask_one * (const_one + step_one))
        + jnp.sum(mask_two * drop_log)
        + jnp.sum(level_mask * (const_two + step_two + top_log))
    )
    total, count = lax.psum((local_total, jnp.sum(mask_one)), ("batch", "rows"))
    coef = -1.0 / (CH * count * math.log(2.0))
    loss = coef * total + 8.0
    grad_top = -coef * level_mask[None] * out_two
    grad_mixed_two, level_two_grads = couple_backward(
        grad_top, coef * level_mask, saved_two, second_params
    )
    grad_input_two, chan_two, lu_two = mix_back_two((grad_mixed_two, coef * jnp.sum(level_mask)))
    grad_drop, grad_prior = prior_back(coef * mask_two)
    prior_low = grad_prior.astype(jnp.bfloat16)
    prior_bias = jnp.sum(prior_low.astype(jnp.float32), axis=(1, 2, 3))
    prior_grad = tap_grads(keep_ext, prior_low)
    prior_ext = stretch_back(prior_low)[:, 1:-1]
    grad_keep = grad_input_two + conv_taps(prior_ext, turn_taps(prior_low_taps))
    vector_two = jnp.concatenate([pack_level(chan_two, lu_two, level_two_grads), prior_bias])
    entry_two = level_two_grads["taps_a"]
    middle_two = level_two_grads["weight_b"]
    exit_two = level_two_grads["taps_c"]
    unfolded = unsqueeze(jnp.concatenate([grad_keep, grad_drop]))
    grad_mixed_one, level_one_grads = couple_backward(
        unfolded, coef * mask_one, saved_one, first_params
    )
    ignored, chan_one, lu_one = mix_back_one((grad_mixed_one, coef * jnp.sum(mask_one)))
    vector_one = pack_level(chan_one, lu_one, level_one_grads)
    entry_one = level_one_grads["taps_a"]
    middle_one = level_one_grads["weight_b"]
    exit_one = level_one_grads["taps_c"]
    (
        vector_one,
        entry_one,
        middle_one,
        exit_one,
        vector_two,
        entry_two,
        middle_two,
        exit_two,
        prior_grad,
    ) = lax.psum(
        (
            vector_one,
            entry_one,
            middle_one,
            exit_one,
            vector_two,
            entry_two,
            middle_two,
            exit_two,
            prior_grad,
        ),
        ("batch", "rows"),
    )
    grads = (
        jnp.concatenate([vector_one, vector_two]),
        jnp.concatenate([entry_one, entry_two], axis=1),
        jnp.stack([middle_one, middle_two]),
        jnp.concatenate([exit_one, exit_two], axis=1),
        prior_grad,
    )
    grad_norm = jnp.sqrt(sum((jnp.sum(grad * grad) for grad in grads)))
    clip = jnp.minimum(1.0, CLIP_NORM / (grad_norm + 1e-06))
    weights = (vectors, entry_taps, middle, exit_taps, prior_taps)
    firsts = (vectors_first, entry_first, middle_first, exit_first, prior_first)
    seconds = (vectors_second, entry_second, middle_second, exit_second, prior_second)
    results = [loss, grad_norm]
    for weight, grad, first, second in zip(weights, grads, firsts, seconds):
        clipped = grad * clip
        updated, second_new = adamw(weight, clipped, first, second)
        results.extend([updated, clipped, second_new])
    results.append(hidden_biases(grads[0] * clip))
    return tuple(results)


def solution(mesh):
    return jax.shard_map(
        on_device,
        mesh=mesh,
        in_specs=(
            P(None, "rows", None, "batch"),
            P("rows", None, "batch"),
            P(),
            P(),
            P(),
            P(),
            P(),
            P(),
            P(),
            P(),
            P(),
            P(),
            P(),
            P(),
            P(),
            P(),
            P(),
        ),
        out_specs=(
            P(),
            P(),
            P(),
            P(),
            P(),
            P(),
            P(),
            P(),
            P(),
            P(),
            P(),
            P(),
            P(),
            P(),
            P(),
            P(),
            P(),
            P(),
        ),
        check_vma=False,
    )
```

profile of v0, /device:TPU:0, one launch (start us, length us, event | category | flops | bytes accessed | tf_op | source)
XLA Modules:
  0.0 892.2 jit_solution(1426610579824177648)
XLA Ops:
  38.3 10.3 %fusion.347 = f32[6,16,128,512]{3,2,1,0:T(8,128)} fusion(bf16[9,512,6]{1,2,0:T(8,128)(2,1)S(1)} %slice_bitcast_fusion.7, bf16[6,2,16,128]{3,0,2,1:T(8,128)(2,1)S(1)} %collective-permute-done.1, bf16[6,4,16,128]{3,0,2,1:T(8,128)(2,1)S(1)} %slice.1746, bf16[6,2,16,128]{3,0,2,1:T(8,128)(2,1)S(1)} %collective-permute-done), kind=kOutput, calls=%fused_computation.561 | convolution fusion | flops 71368704 | bytes 25436160 | tf_op jit(solution)/shard_map/dot_general | solution.py:41
  48.6 10.2 %fusion.349 = f32[6,16,128,512]{3,2,1,0:T(8,128)} fusion(bf16[9,512,6]{1,2,0:T(8,128)(2,1)S(1)} %slice_bitcast_fusion.7, bf16[6,2,16,128]{3,0,2,1:T(8,128)(2,1)S(1)} %collective-permute-done.1, bf16[6,4,16,128]{3,0,2,1:T(8,128)(2,1)S(1)} %slice.1746, bf16[6,2,16,128]{3,0,2,1:T(8,128)(2,1)S(1)} %collective-permute-done), kind=kOutput, calls=%fused_computation.565 | convolution fusion | flops 76087296 | bytes 25436160 | tf_op jit(solution)/shard_map/dot_general | solution.py:41
  58.8 10.1 %fusion.352 = f32[6,16,128,512]{3,2,1,0:T(8,128)} fusion(bf16[9,512,6]{1,2,0:T(8,128)(2,1)S(1)} %slice_bitcast_fusion.7, bf16[6,2,16,128]{3,0,2,1:T(8,128)(2,1)S(1)} %collective-permute-done.1, bf16[6,4,16,128]{3,0,2,1:T(8,128)(2,1)S(1)} %slice.1746, bf16[6,2,16,128]{3,0,2,1:T(8,128)(2,1)S(1)} %collective-permute-done), kind=kOutput, calls=%fused_computation.572 | convolution fusion | flops 71368704 | bytes 25436160 | tf_op jit(solution)/shard_map/dot_general | solution.py:41
  68.9 10.1 %fusion.351 = f32[6,16,128,512]{3,2,1,0:T(8,128)} fusion(bf16[9,512,6]{1,2,0:T(8,128)(2,1)S(1)} %slice_bitcast_fusion.7, bf16[6,2,16,128]{3,0,2,1:T(8,128)(2,1)S(1)} %collective-permute-done.1, bf16[6,4,16,128]{3,0,2,1:T(8,128)(2,1)S(1)} %slice.1746, bf16[6,2,16,128]{3,0,2,1:T(8,128)(2,1)S(1)} %collective-permute-done), kind=kOutput, calls=%fused_computation.569 | convolution fusion | flops 71368704 | bytes 25436160 | tf_op jit(solution)/shard_map/dot_general | solution.py:41
  79.0 10.2 %fusion.350 = f32[6,16,128,512]{3,2,1,0:T(8,128)} fusion(bf16[9,512,6]{1,2,0:T(8,128)(2,1)S(1)} %slice_bitcast_fusion.7, bf16[6,2,16,128]{3,0,2,1:T(8,128)(2,1)S(1)} %collective-permute-done.1, bf16[6,4,16,128]{3,0,2,1:T(8,128)(2,1)S(1)} %slice.1746, bf16[6,2,16,128]{3,0,2,1:T(8,128)(2,1)S(1)} %collective-permute-done), kind=kOutput, calls=%fused_computation.567 | convolution fusion | flops 71368704 | bytes 25436160 | tf_op jit(solution)/shard_map/dot_general | solution.py:41
  89.1 10.1 %fusion.348 = f32[6,16,128,512]{3,2,1,0:T(8,128)} fusion(bf16[9,512,6]{1,2,0:T(8,128)(2,1)S(1)} %slice_bitcast_fusion.7, bf16[6,2,16,128]{3,0,2,1:T(8,128)(2,1)S(1)} %collective-permute-done.1, bf16[6,4,16,128]{3,0,2,1:T(8,128)(2,1)S(1)} %slice.1746, bf16[6,2,16,128]{3,0,2,1:T(8,128)(2,1)S(1)} %collective-permute-done), kind=kOutput, calls=%fused_computation.563 | convolution fusion | flops 71368704 | bytes 25436160 | tf_op jit(solution)/shard_map/dot_general | solution.py:41
  99.2 10.1 %fusion.222 = f32[6,16,128,512]{3,2,1,0:T(8,128)} fusion(bf16[6,2,16,128]{3,0,2,1:T(8,128)(2,1)S(1)} %collective-permute-done.1, bf16[6,4,16,128]{3,0,2,1:T(8,128)(2,1)S(1)} %slice.1746, bf16[9,512,6]{1,2,0:T(8,128)(2,1)S(1)} %slice_bitcast_fusion.7), kind=kOutput, calls=%fused_computation.332 | convolution fusion | flops 75571200 | bytes 25370624 | tf_op jit(solution)/shard_map/dot_general | solution.py:41
  109.4 10.3 %fusion.218 = f32[6,16,128,512]{3,2,1,0:T(8,128)} fusion(bf16[6,4,16,128]{3,0,2,1:T(8,128)(2,1)S(1)} %slice.1746, bf16[6,2,16,128]{3,0,2,1:T(8,128)(2,1)S(1)} %collective-permute-done, bf16[9,512,6]{1,2,0:T(8,128)(2,1)S(1)} %slice_bitcast_fusion.7), kind=kOutput, calls=%fused_computation.328 | convolution fusion | flops 75571200 | bytes 25370624 | tf_op jit(solution)/shard_map/dot_general | solution.py:41
  119.7 65.1 %fusion.3 = bf16[512,6,16,128]{0,3,2,1:T(8,128)(2,1)} fusion(f32[512]{0:T(512)S(1)} %get-tuple-element.133, f32[6,16,128,512]{3,2,1,0:T(8,128)} %fusion.222, f32[6,16,128,512]{3,2,1,0:T(8,128)} %fusion.347, f32[6,16,128,512]{3,2,1,0:T(8,128)} %fusion.348, f32[6,16,128,512]{3,2,1,0:T(8,128)} %fusion.349, f32[6,16,128,512]{3,2,1,0:T(8,128)} %fusion.350, ...), kind=kOutput, calls=%fused_computation.9 | convolution fusion | flops 140574720 | bytes 214181888 | tf_op jit(solution)/shard_map/dot_general | solution.py:41
  184.7 12.1 %fusion.2 = bf16[512,6,16,128]{0,3,2,1:T(8,128)(2,1)S(1)} fusion(f32[6]{0:T(128)S(1)} %and_convert_fusion.1, f32[512]{0:T(512)S(1)} %get-tuple-element.132, bf16[512,6,16,128]{0,3,2,1:T(8,128)(2,1)} %fusion.3, bf16[2,512,512]{2,1,0:T(8,128)(2,1)S(1)} %convert.15), kind=kOutput, calls=%fused_computation.8 | convolution fusion | flops 6467616768 | bytes 25692672 | tf_op jit(solution)/shard_map/dot_general | solution.py:155
  218.1 44.1 %psum.77 = f32[]{:T(128)} all-reduce(f32[]{:T(128)} %get-tuple-element.47), channel_id=1, replica_groups=mesh['batch'=8,'rows'=4] {'batch','rows'}, use_global_device_ids=true, to_apply=%region_1.2 | all-reduce | flops 1 | bytes 8 | tf_op jit(solution)/shard_map/psum | solution.py:279
  308.6 19.3 %fusion.21 = bf16[512,4,8,128]{0,3,2,1:T(8,128)(2,1)} fusion(f32[512]{0:T(512)} %get-tuple-element.130, f32[4,8,128,512]{3,2,1,0:T(8,128)} %fusion.272, f32[4,8,128,512]{3,2,1,0:T(8,128)S(1)} %fusion.324, f32[4,8,128,512]{3,2,1,0:T(8,128)} %fusion.325, f32[4,8,128,512]{3,2,1,0:T(8,128)S(1)} %fusion.326, f32[4,8,128,512]{3,2,1,0:T(8,128)} %fusion.327, ...), kind=kOutput, calls=%fused_computation.45 | convolution fusion | flops 67551232 | bytes 71518208 | tf_op jit(solution)/shard_map/dot_general | solution.py:41
  327.9 4.8 fusion.20
  351.8 5.3 collective-permute-start.8
  402.4 32.5 %fusion.13 = bf16[512,4,8,128]{0,3,2,1:T(8,128)(2,1)} fusion(f32[4,8,128,512]{3,2,1,0:T(8,128)} %fusion.238, f32[4,8,128,512]{3,2,1,0:T(8,128)} %fusion.306, f32[4,8,128,512]{3,2,1,0:T(8,128)} %fusion.307, f32[4,8,128,512]{3,2,1,0:T(8,128)S(1)} %fusion.308, f32[4,8,128,512]{3,2,1,0:T(8,128)} %fusion.309, f32[4,8,128,512]{3,2,1,0:T(8,128)} %fusion.310, ...), kind=kOutput, calls=%fused_computation.27 | convolution fusion | flops 112033792 | bytes 75816960 | tf_op jit(solution)/shard_map/dot_general | solution.py:41
  441.3 6.1 fusion.12
  498.3 10.6 %fusion.318 = f32[6,16,128,512]{3,2,1,0:T(8,128)} fusion(bf16[9,512,12]{1,2,0:T(8,128)(2,1)S(1)} %copy-done.31, bf16[12,2,16,128]{3,0,2,1:T(8,128)(2,1)S(1)} %collective-permute-done.11, bf16[12,4,16,128]{3,0,2,1:T(8,128)(2,1)S(1)} %get-tuple-element.81, bf16[12,2,16,128]{3,0,2,1:T(8,128)(2,1)S(1)} %collective-permute-done.10), kind=kOutput, calls=%fused_computation.481 | convolution fusion | flops 152174592 | bytes 25706496 | tf_op jit(solution)/shard_map/dot_general | solution.py:41
  508.9 10.1 %fusion.321 = f32[6,16,128,512]{3,2,1,0:T(8,128)} fusion(bf16[9,512,12]{1,2,0:T(8,128)(2,1)S(1)} %copy-done.31, bf16[12,2,16,128]{3,0,2,1:T(8,128)(2,1)S(1)} %collective-permute-done.11, bf16[12,4,16,128]{3,0,2,1:T(8,128)(2,1)S(1)} %get-tuple-element.81, bf16[12,2,16,128]{3,0,2,1:T(8,128)(2,1)S(1)} %collective-permute-done.10), kind=kOutput, calls=%fused_computation.488 | convolution fusion | flops 142737408 | bytes 25706496 | tf_op jit(solution)/shard_map/dot_general | solution.py:41
  519.0 10.1 %fusion.320 = f32[6,16,128,512]{3,2,1,0:T(8,128)} fusion(bf16[9,512,12]{1,2,0:T(8,128)(2,1)S(1)} %copy-done.31, bf16[12,2,16,128]{3,0,2,1:T(8,128)(2,1)S(1)} %collective-permute-done.11, bf16[12,4,16,128]{3,0,2,1:T(8,128)(2,1)S(1)} %get-tuple-element.81, bf16[12,2,16,128]{3,0,2,1:T(8,128)(2,1)S(1)} %collective-permute-done.10), kind=kOutput, calls=%fused_computation.485 | convolution fusion | flops 142737408 | bytes 25706496 | tf_op jit(solution)/shard_map/dot_general | solution.py:41
  529.1 10.1 %fusion.319 = f32[6,16,128,512]{3,2,1,0:T(8,128)} fusion(bf16[9,512,12]{1,2,0:T(8,128)(2,1)S(1)} %copy-done.31, bf16[12,2,16,128]{3,0,2,1:T(8,128)(2,1)S(1)} %collective-permute-done.11, bf16[12,4,16,128]{3,0,2,1:T(8,128)(2,1)S(1)} %get-tuple-element.81, bf16[12,2,16,128]{3,0,2,1:T(8,128)(2,1)S(1)} %collective-permute-done.10), kind=kOutput, calls=%fused_computation.483 | convolution fusion | flops 142737408 | bytes 25706496 | tf_op jit(solution)/shard_map/dot_general | solution.py:41
  539.2 10.1 %fusion.317 = f32[6,16,128,512]{3,2,1,0:T(8,128)} fusion(bf16[9,512,12]{1,2,0:T(8,128)(2,1)S(1)} %copy-done.31, bf16[12,2,16,128]{3,0,2,1:T(8,128)(2,1)S(1)} %collective-permute-done.11, bf16[12,4,16,128]{3,0,2,1:T(8,128)(2,1)S(1)} %get-tuple-element.81, bf16[12,2,16,128]{3,0,2,1:T(8,128)(2,1)S(1)} %collective-permute-done.10), kind=kOutput, calls=%fused_computation.479 | convolution fusion | flops 142737408 | bytes 25706496 | tf_op jit(solution)/shard_map/dot_general | solution.py:41
  549.3 10.0 %fusion.316 = f32[6,16,128,512]{3,2,1,0:T(8,128)} fusion(bf16[9,512,12]{1,2,0:T(8,128)(2,1)S(1)} %copy-done.31, bf16[12,2,16,128]{3,0,2,1:T(8,128)(2,1)S(1)} %collective-permute-done.11, bf16[12,4,16,128]{3,0,2,1:T(8,128)(2,1)S(1)} %get-tuple-element.81, bf16[12,2,16,128]{3,0,2,1:T(8,128)(2,1)S(1)} %collective-permute-done.10), kind=kOutput, calls=%fused_computation.477 | convolution fusion | flops 142737408 | bytes 25706496 | tf_op jit(solution)/shard_map/dot_general | solution.py:41
  559.3 10.1 %fusion.186 = f32[6,16,128,512]{3,2,1,0:T(8,128)} fusion(bf16[12,2,16,128]{3,0,2,1:T(8,128)(2,1)S(1)} %collective-permute-done.11, bf16[12,4,16,128]{3,0,2,1:T(8,128)(2,1)S(1)} %get-tuple-element.81, bf16[9,512,12]{1,2,0:T(8,128)(2,1)S(1)} %copy-done.31), kind=kOutput, calls=%fused_computation.276 | convolution fusion | flops 151142400 | bytes 25575424 | tf_op jit(solution)/shard_map/dot_general | solution.py:41
  569.5 10.2 %fusion.182 = f32[6,16,128,512]{3,2,1,0:T(8,128)} fusion(bf16[12,4,16,128]{3,0,2,1:T(8,128)(2,1)S(1)} %get-tuple-element.81, bf16[12,2,16,128]{3,0,2,1:T(8,128)(2,1)S(1)} %collective-permute-done.10, bf16[9,512,12]{1,2,0:T(8,128)(2,1)S(1)} %copy-done.31), kind=kOutput, calls=%fused_computation.272 | convolution fusion | flops 151142400 | bytes 25575424 | tf_op jit(solution)/shard_map/dot_general | solution.py:41
  579.7 68.6 %fusion.1 = bf16[512,6,16,128]{0,3,2,1:T(8,128)(2,1)} fusion(f32[6,16,128,512]{3,2,1,0:T(8,128)} %fusion.186, f32[6,16,128,512]{3,2,1,0:T(8,128)} %fusion.316, f32[6,16,128,512]{3,2,1,0:T(8,128)} %fusion.317, f32[6,16,128,512]{3,2,1,0:T(8,128)} %fusion.318, f32[6,16,128,512]{3,2,1,0:T(8,128)} %fusion.319, f32[6,16,128,512]{3,2,1,0:T(8,128)} %fusion.320, ...), kind=kOutput, calls=%fused_computation.3 | convolution fusion | flops 211943424 | bytes 227033088 | tf_op jit(solution)/shard_map/dot_general | solution.py:41
  648.2 11.3 %fusion.40 = f32[1,512,512]{2,1,0:T(8,128)} fusion(bf16[512,6,16,128]{0,3,2,1:T(8,128)(2,1)} %fusion.1, bf16[512,6,16,128]{0,3,2,1:T(8,128)(2,1)} %fusion.3), kind=kOutput, calls=%fused_computation.65 | convolution fusion | flops 4294967296 | bytes 22020096 | tf_op jit(solution)/shard_map/dot_general | solution.py:187
  659.6 16.3 %fusion = bf16[512,6,16,128]{0,3,2,1:T(8,128)(2,1)} fusion(bf16[512,6,16,128]{0,3,2,1:T(8,128)(2,1)} %fusion.3, bf16[512,6,16,128]{0,3,2,1:T(8,128)(2,1)} %fusion.1, bf16[2,512,512]{2,1,0:T(8,128)(2,1)S(1)} %copy-done.22), kind=kOutput, calls=%fused_computation.1 | convolution fusion | flops 6461325312 | bytes 38273024 | tf_op jit(solution)/shard_map/dot_general | solution.py:193
  675.9 5.8 fusion.344
  681.7 5.8 fusion.343
  721.7 5.0 convert_reduce_fusion.1
  726.8 42.3 %all-reduce.28 = (f32[]{:T(128)}, f32[1744]{0:T(1024)S(1)}, f32[1216]{0:T(1024)S(1)}, f32[9,48,24]{1,2,0:T(8,128)S(1)}) all-reduce(f32[]{:T(128)S(6)} %add.843, f32[1744]{0:T(1024)S(1)} %copy-done.57, f32[1216]{0:T(1024)S(1)} %concatenate.123, f32[9,48,24]{1,2,0:T(8,128)} %fusion.151), channel_id=1, replica_groups=mesh['batch'=8,'rows'=4] {'batch','rows'}, use_global_device_ids=true, to_apply=%region_14.15 | all-reduce | flops 13329 | bytes 106632 | tf_op jit(solution)/shard_map/psum | solution.py:279
  771.0 86.9 %all-reduce.32.cloned.1.call-done = (f32[9,12,512]{2,1,0:T(8,128)}, f32[9,6,512]{2,1,0:T(8,128)}, f32[1,512,512]{2,1,0:T(8,128)}, f32[1,512,512]{2,1,0:T(8,128)}...) async-done(((f32[9,12,512]{2,1,0:T(8,128)}, f32[9,6,512]{2,1,0:T(8,128)}, f32[1,512,512]{2,1,0:T(8,128)}, f32[1,512,512]{2,1,0:T(8,128)}, f32[9,24,512]{2,1,0:T(8,128)}, ...) | async-done | bytes 3092496 | tf_op jit(solution)/shard_map/psum | solution.py:316
  (443 shorter events, 269.6 us)
Async XLA Ops:
  7.2 850.7 %all-reduce.32.cloned.1.call-start = ((), (), s32[]{:S(2)}) async-start(), calls=%async_computation | async-start | bytes 6553600 | tf_op jit(solution)/shard_map/psum | solution.py:316
  14.7 262.6 %copy-start.4 = (bf16[6,4,16,128]{3,0,2,1:T(8,128)(2,1)}, bf16[6,4,16,128]{3,0,2,1:T(8,128)(2,1)S(1)}, u32[]{:S(2)}) copy-start(bf16[6,4,16,128]{3,0,2,1:T(8,128)(2,1)S(1)} %slice.1746) | copy-start | bytes 294916
  14.7 23.5 %collective-permute-start = (bf16[6,2,16,128]{3,0,2,1:T(8,128)(2,1)S(1)}, bf16[6,2,16,128]{3,0,2,1:T(8,128)(2,1)S(1)}, u32[]{:S(2)}, u32[]{:S(2)}) collective-permute-start(bf16[6,2,16,128]{3,0,2,1:T(8,128)(2,1)S(1)} %get-tuple-element.110), channel_id=1, source_target_pairs={{0,1},{1,2},{2,3},{4,5},{5,6},{6,7},{8,9},{9,10},{10,11},{12,13},{... | collective-permute-start | bytes 147464 | tf_op jit(solution)/shard_map/ppermute | solution.py:27
  17.1 21.2 %collective-permute-start.1 = (bf16[6,2,16,128]{3,0,2,1:T(8,128)(2,1)S(1)}, bf16[6,2,16,128]{3,0,2,1:T(8,128)(2,1)S(1)}, u32[]{:S(2)}, u32[]{:S(2)}) collective-permute-start(bf16[6,2,16,128]{3,0,2,1:T(8,128)(2,1)S(1)} %get-tuple-element.111), channel_id=1, source_target_pairs={{1,0},{2,1},{3,2},{5,4},{6,5},{7,6},{9,8},{10,9},{11,10},{13,12},{... | collective-permute-start | bytes 147464 | tf_op jit(solution)/shard_map/ppermute | solution.py:28
  22.5 26.1 %copy-start.19 = (bf16[9,512,12]{1,2,0:T(8,128)(2,1)}, bf16[9,512,12]{1,2,0:T(8,128)(2,1)S(1)}, u32[]{:S(2)}) copy-start(bf16[9,512,12]{1,2,0:T(8,128)(2,1)S(1)} %slice_bitcast_fusion.6) | copy-start | bytes 331780
  36.3 148.4 %copy-start.21 = (bf16[2,512,512]{2,1,0:T(8,128)(2,1)}, bf16[2,512,512]{2,1,0:T(8,128)(2,1)S(1)}, u32[]{:S(2)}) copy-start(bf16[2,512,512]{2,1,0:T(8,128)(2,1)S(1)} %convert.15) | copy-start | bytes 3145732
  38.3 239.1 %copy-start.9 = (bf16[6,2,16,128]{3,0,2,1:T(8,128)(2,1)}, bf16[6,2,16,128]{3,0,2,1:T(8,128)(2,1)S(1)}, u32[]{:S(2)}) copy-start(bf16[6,2,16,128]{3,0,2,1:T(8,128)(2,1)S(1)} %collective-permute-done) | copy-start | bytes 147460
  38.3 239.1 %copy-start.7 = (bf16[6,2,16,128]{3,0,2,1:T(8,128)(2,1)}, bf16[6,2,16,128]{3,0,2,1:T(8,128)(2,1)S(1)}, u32[]{:S(2)}) copy-start(bf16[6,2,16,128]{3,0,2,1:T(8,128)(2,1)S(1)} %collective-permute-done.1) | copy-start | bytes 147460
  196.8 18.2 %copy-start = (bf16[512,6,16,128]{0,3,2,1:T(8,128)(2,1)}, bf16[512,6,16,128]{0,3,2,1:T(8,128)(2,1)S(1)}, u32[]{:S(2)}) copy-start(bf16[512,6,16,128]{0,3,2,1:T(8,128)(2,1)S(1)} %fusion.2) | copy-start | bytes 37748740
  214.9 55.3 %copy-start.43 = (f32[24,24]{1,0:T(8,128)S(1)}, f32[24,24]{1,0:T(8,128)}, u32[]{:S(2)}) copy-start(f32[24,24]{1,0:T(8,128)} %rev.28) | copy-start | bytes 6916
  214.9 55.3 %copy-start.59 = (f32[24]{0:T(128)S(1)}, f32[24]{0:T(128)}, u32[]{:S(2)}) copy-start(f32[24]{0:T(128)} %get-tuple-element.127) | copy-start | bytes 292
  214.9 55.3 %copy-start.62 = (f32[24]{0:T(128)S(1)}, f32[24]{0:T(128)}, u32[]{:S(2)}) copy-start(f32[24]{0:T(128)} %get-tuple-element.129) | copy-start | bytes 292
  214.9 61.2 %copy-start.49 = (f32[2,8,128]{2,1,0:T(8,128)S(1)}, f32[2,8,128]{2,1,0:T(8,128)}, u32[]{:S(2)}) copy-start(f32[2,8,128]{2,1,0:T(8,128)} %reduce_min.9) | copy-start | bytes 24580
  215.0 64.1 %copy-start.20 = (bf16[9,512,12]{1,2,0:T(8,128)(2,1)S(1)}, bf16[9,512,12]{1,2,0:T(8,128)(2,1)}, u32[]{:S(2)}) copy-start(bf16[9,512,12]{1,2,0:T(8,128)(2,1)} %copy-done.19) | copy-start | bytes 331780
  265.2 73.6 %collective-permute-start.3 = (bf16[24,2,8,128]{3,0,2,1:T(8,128)(2,1)S(1)}, bf16[24,2,8,128]{3,0,2,1:T(8,128)(2,1)}, u32[]{:S(2)}, u32[]{:S(2)}) collective-permute-start(bf16[24,2,8,128]{3,0,2,1:T(8,128)(2,1)S(1)} %copy.686), channel_id=1, source_target_pairs={{1,0},{2,1},{3,2},{5,4},{6,5},{7,6},{9,8},{10,9},{11,10},{13,12},{... | collective-permute-start | bytes 294920 | tf_op jit(solution)/shard_map/ppermute | solution.py:28
  266.5 72.3 %collective-permute-start.2 = (bf16[24,2,8,128]{3,0,2,1:T(8,128)(2,1)S(1)}, bf16[24,2,8,128]{3,0,2,1:T(8,128)(2,1)}, u32[]{:S(2)}, u32[]{:S(2)}) collective-permute-start(bf16[24,2,8,128]{3,0,2,1:T(8,128)(2,1)S(1)} %copy.686), channel_id=1, source_target_pairs={{0,1},{1,2},{2,3},{4,5},{5,6},{6,7},{8,9},{9,10},{10,11},{12,13},{... | collective-permute-start | bytes 294920 | tf_op jit(solution)/shard_map/ppermute | solution.py:27
  270.6 8.4 collective-permute-start.5
  271.9 7.1 collective-permute-start.4
  340.7 24.6 %copy-start.39 = (bf16[9,24,48]{2,1,0:T(8,128)(2,1)S(1)}, bf16[9,24,48]{2,1,0:T(8,128)(2,1)}, u32[]{:S(2)}) copy-start(bf16[9,24,48]{2,1,0:T(8,128)(2,1)} %reverse_bitcast_fusion.4) | copy-start | bytes 62212
  344.0 24.5 %collective-permute-start.7 = (bf16[24,2,8,128]{3,0,2,1:T(8,128)(2,1)S(1)}, bf16[24,2,8,128]{3,0,2,1:T(8,128)(2,1)S(1)}, u32[]{:S(2)}, u32[]{:S(2)}) collective-permute-start(bf16[24,2,8,128]{3,0,2,1:T(8,128)(2,1)S(1)} %get-tuple-element.89), channel_id=1, source_target_pairs={{1,0},{2,1},{3,2},{5,4},{6,5},{7,6},{9,8},{10,9},{11,10},{13,12},{... | collective-permute-start | bytes 294920 | tf_op jit(solution)/shard_map/ppermute | solution.py:28
  345.3 24.0 %collective-permute-start.6 = (bf16[24,2,8,128]{3,0,2,1:T(8,128)(2,1)S(1)}, bf16[24,2,8,128]{3,0,2,1:T(8,128)(2,1)S(1)}, u32[]{:S(2)}, u32[]{:S(2)}) collective-permute-start(bf16[24,2,8,128]{3,0,2,1:T(8,128)(2,1)S(1)} %get-tuple-element.89), channel_id=1, source_target_pairs={{0,1},{1,2},{2,3},{4,5},{5,6},{6,7},{8,9},{9,10},{10,11},{12,13},{... | collective-permute-start | bytes 294920 | tf_op jit(solution)/shard_map/ppermute | solution.py:27
  350.5 123.1 %collective-permute-start.9 = (bf16[48,2,8,128]{3,0,2,1:T(8,128)(2,1)S(1)}, bf16[48,2,8,128]{3,0,2,1:T(8,128)(2,1)}, u32[]{:S(2)}, u32[]{:S(2)}) collective-permute-start(bf16[48,2,8,128]{3,0,2,1:T(8,128)(2,1)S(1)} %get-tuple-element.83), channel_id=1, source_target_pairs={{1,0},{2,1},{3,2},{5,4},{6,5},{7,6},{9,8},{10,9},{11,10},{13,12},{... | collective-permute-start | bytes 589832 | tf_op jit(solution)/shard_map/ppermute | solution.py:28
  351.8 121.8 %collective-permute-start.8 = (bf16[48,2,8,128]{3,0,2,1:T(8,128)(2,1)S(1)}, bf16[48,2,8,128]{3,0,2,1:T(8,128)(2,1)}, u32[]{:S(2)}, u32[]{:S(2)}) collective-permute-start(bf16[48,2,8,128]{3,0,2,1:T(8,128)(2,1)S(1)} %get-tuple-element.83), channel_id=1, source_target_pairs={{0,1},{1,2},{2,3},{4,5},{5,6},{6,7},{8,9},{9,10},{10,11},{12,13},{... | collective-permute-start | bytes 589832 | tf_op jit(solution)/shard_map/ppermute | solution.py:27
  466.9 12.4 %copy-start.41 = (f32[4,16,128]{2,1,0:T(8,128)S(1)}, f32[4,16,128]{2,1,0:T(8,128)}, u32[]{:S(2)}) copy-start(f32[4,16,128]{2,1,0:T(8,128)} %broadcast_multiply_fusion.2) | copy-start | bytes 98308
  471.5 17.4 %slice-start = ((s8[12582912]{0:T(1024)(128)(4,1)}), s8[4194304]{0:T(1024)(128)(4,1)S(1)}, s32[]{:S(2)}) async-start(s8[12582912]{0:T(1024)(128)(4,1)} %bitcast.1259), calls=%async_computation.1 | async-start | bytes 8388608
  484.6 13.7 %collective-permute-start.10 = (bf16[12,2,16,128]{3,0,2,1:T(8,128)(2,1)S(1)}, bf16[12,2,16,128]{3,0,2,1:T(8,128)(2,1)S(1)}, u32[]{:S(2)}, u32[]{:S(2)}) collective-permute-start(bf16[12,2,16,128]{3,0,2,1:T(8,128)(2,1)S(1)} %get-tuple-element.103), channel_id=1, source_target_pairs={{0,1},{1,2},{2,3},{4,5},{5,6},{6,7},{8,9},{9,10},{10,11},{12,13},{... | collective-permute-start | bytes 294920 | tf_op jit(solution)/shard_map/ppermute | solution.py:27
  487.6 10.7 %collective-permute-start.11 = (bf16[12,2,16,128]{3,0,2,1:T(8,128)(2,1)S(1)}, bf16[12,2,16,128]{3,0,2,1:T(8,128)(2,1)S(1)}, u32[]{:S(2)}, u32[]{:S(2)}) collective-permute-start(bf16[12,2,16,128]{3,0,2,1:T(8,128)(2,1)S(1)} %get-tuple-element.104), channel_id=1, source_target_pairs={{1,0},{2,1},{3,2},{5,4},{6,5},{7,6},{9,8},{10,9},{11,10},{13,12},{... | collective-permute-start | bytes 294920 | tf_op jit(solution)/shard_map/ppermute | solution.py:28
  659.6 16.3 %copy-start.38 = (bf16[9,6,512]{2,1,0:T(8,128)(2,1)S(1)}, bf16[9,6,512]{2,1,0:T(8,128)(2,1)}, u32[]{:S(2)}) copy-start(bf16[9,6,512]{2,1,0:T(8,128)(2,1)} %reverse_bitcast_fusion.3) | copy-start | bytes 165892
  675.9 11.6 %copy-start.1 = (bf16[512,6,16,128]{0,3,2,1:T(8,128)(2,1)S(1)}, bf16[512,6,16,128]{0,3,2,1:T(8,128)(2,1)}, u32[]{:S(2)}) copy-start(bf16[512,6,16,128]{0,3,2,1:T(8,128)(2,1)} %fusion) | copy-start | bytes 37748740
  721.6 151.8 %copy-start.18 = (f32[9,18,512]{2,1,0:T(8,128)S(1)}, f32[9,18,512]{2,1,0:T(8,128)}, u32[]{:S(2)}) copy-start(f32[9,18,512]{2,1,0:T(8,128)} %param.26) | copy-start | bytes 995332
  721.6 154.3 %copy-start.15 = (f32[9,36,512]{2,1,0:T(8,128)S(1)}, f32[9,36,512]{2,1,0:T(8,128)}, u32[]{:S(2)}) copy-start(f32[9,36,512]{2,1,0:T(8,128)} %param.32) | copy-start | bytes 1990660
  857.9 15.5 %copy-start.30 = (f32[9,6,512]{2,1,0:T(8,128)S(1)}, f32[9,6,512]{2,1,0:T(8,128)}, u32[]{:S(2)}) copy-start(f32[9,6,512]{2,1,0:T(8,128)} %get-tuple-element.60) | copy-start | bytes 331780
  (63 other events, 303.9 us)
Sparse Core Ops, SparseCore 0:
  717.1 140.8 all-reduce.31
where the time goes:
time: 897 us; the launch traced here: 892 us
  matrix products  587 us (65%)
  waiting for transfers between devices  87 us (10%)
  blocking collectives  86.4 us (10%)
  other arithmetic  51.2 us (6%)
  starting transfers between devices  30.5 us (3%)
  between operations  28.8 us (3%)
  local copies, waits for them, and re-layouts  21.7 us (2%)
    dot_general x90, matrix products, conv_taps(): lax.dot_general(weight[tap_index], window, (((1,), (0,)), ((), ())), pref...  477 us
    psum x1, waiting for transfers between devices, on_device(): lax.psum((vector_one, entry_one, middle_one, exit_one, vector_two, entry_...  86.9 us
    psum x2, blocking collectives, on_device(): total, count = lax.psum((local_total, jnp.sum(mask_one)), ('batch', 'rows'))  86.4 us
    dot_general x45, matrix products, tap_grads(): lax.dot_general(grad, window, (((1, 2, 3), (1, 2, 3)), ((), ())), preferr...  48.2 us
    ppermute x6, starting transfers between devices, padded_2(): before = lax.ppermute(last, axis, up)  22.7 us
    dot_general x2, matrix products, couple_backward(): lax.dot_general(params['weight_b'], pre_two_low, (((0,), (0,)), ((), ()))...  22.3 us
  transfers between devices with their start and end apart: 13, of which 1 were waited for; matrix products, arithmetic and copies ran while one was open for 24% of the time, Pallas kernels for 0%

commit v1 on v0

--- a/solution.py
+++ b/solution.py
@@ -276,7 +276,7 @@
         + jnp.sum(mask_two * drop_log)
         + jnp.sum(level_mask * (const_two + step_two + top_log))
     )
-    total, count = lax.psum((local_total, jnp.sum(mask_one)), ("batch", "rows"))
+    total, count = lax.psum(lax.psum((local_total, jnp.sum(mask_one)), "rows"), "batch")
     coef = -1.0 / (CH * count * math.log(2.0))
     loss = coef * total + 8.0
     grad_top = -coef * level_mask[None] * out_two

time: 897 us -> 868 us (0.968)
  blocking collectives: 86.4 us -> 69.3 us
  matrix products: 587 us -> 577 us
    psum x2 -> x3, blocking collectives: 86.4 us -> 69.3 us  [the longest x1 39 us: on_device(): lax.psum((vector_one, entry_one, middle_one, exit_one, vector_two, entry_...]
    dot_general x90, matrix products: 477 us -> 462 us  [conv_taps(): lax.dot_general(weight[tap_index], window, (((1,), (0,)), ((), ())), pref...]
where the time goes in v1:
time: 868 us; the launch traced here: 864 us
  matrix products  577 us (66%)
  waiting for transfers between devices  89.9 us (10%)
  blocking collectives  69.3 us (8%)
  other arithmetic  48.9 us (6%)
  starting transfers between devices  31.7 us (4%)
  between operations  28.7 us (3%)
  local copies, waits for them, and re-layouts  18.7 us (2%)
    dot_general x90, matrix products, conv_taps(): lax.dot_general(weight[tap_index], window, (((1,), (0,)), ((), ())), pref...  462 us
    psum x1, waiting for transfers between devices, on_device(): lax.psum((vector_one, entry_one, middle_one, exit_one, vector_two, entry_...  89.8 us
    dot_general x45, matrix products, tap_grads(): lax.dot_general(grad, window, (((1, 2, 3), (1, 2, 3)), ((), ())), preferr...  53.7 us
    psum x1, blocking collectives, on_device(): lax.psum((vector_one, entry_one, middle_one, exit_one, vector_two, entry_...  39 us
    ppermute x6, starting transfers between devices, padded_2(): before = lax.ppermute(last, axis, up)  23.7 us
    dot_general x2, matrix products, couple_backward(): lax.dot_general(params['weight_b'], pre_two_low, (((0,), (0,)), ((), ()))...  22.3 us
    psum x1, blocking collectives, on_device(): lax.psum(lax.psum((local_total, jnp.sum(mask_one)), 'rows'), 'batch')  22.3 us
  transfers between devices with their start and end apart: 13, of which 1 were waited for; matrix products, arithmetic and copies ran while one was open for 24% of the time, Pallas kernels for 0%

profile of v1, /device:TPU:0, one launch (start us, length us, event | category | flops | bytes accessed | tf_op | source)
XLA Modules:
  0.0 864.0 jit_solution(16038635472626152014)
XLA Ops:
  40.2 10.3 %fusion.347 = f32[6,16,128,512]{3,2,1,0:T(8,128)} fusion(bf16[9,512,6]{1,2,0:T(8,128)(2,1)S(1)} %slice_bitcast_fusion.7, bf16[6,2,16,128]{3,0,2,1:T(8,128)(2,1)S(1)} %collective-permute-done.1, bf16[6,4,16,128]{3,0,2,1:T(8,128)(2,1)S(1)} %slice.1746, bf16[6,2,16,128]{3,0,2,1:T(8,128)(2,1)S(1)} %collective-permute-done), kind=kOutput, calls=%fused_computation.561 | convolution fusion | flops 71368704 | bytes 25436160 | tf_op jit(solution)/shard_map/dot_general | solution.py:41
  50.5 10.2 %fusion.349 = f32[6,16,128,512]{3,2,1,0:T(8,128)} fusion(bf16[9,512,6]{1,2,0:T(8,128)(2,1)S(1)} %slice_bitcast_fusion.7, bf16[6,2,16,128]{3,0,2,1:T(8,128)(2,1)S(1)} %collective-permute-done.1, bf16[6,4,16,128]{3,0,2,1:T(8,128)(2,1)S(1)} %slice.1746, bf16[6,2,16,128]{3,0,2,1:T(8,128)(2,1)S(1)} %collective-permute-done), kind=kOutput, calls=%fused_computation.565 | convolution fusion | flops 76087296 | bytes 25436160 | tf_op jit(solution)/shard_map/dot_general | solution.py:41
  60.7 10.1 %fusion.352 = f32[6,16,128,512]{3,2,1,0:T(8,128)} fusion(bf16[9,512,6]{1,2,0:T(8,128)(2,1)S(1)} %slice_bitcast_fusion.7, bf16[6,2,16,128]{3,0,2,1:T(8,128)(2,1)S(1)} %collective-permute-done.1, bf16[6,4,16,128]{3,0,2,1:T(8,128)(2,1)S(1)} %slice.1746, bf16[6,2,16,128]{3,0,2,1:T(8,128)(2,1)S(1)} %collective-permute-done), kind=kOutput, calls=%fused_computation.572 | convolution fusion | flops 71368704 | bytes 25436160 | tf_op jit(solution)/shard_map/dot_general | solution.py:41
  70.8 10.1 %fusion.351 = f32[6,16,128,512]{3,2,1,0:T(8,128)} fusion(bf16[9,512,6]{1,2,0:T(8,128)(2,1)S(1)} %slice_bitcast_fusion.7, bf16[6,2,16,128]{3,0,2,1:T(8,128)(2,1)S(1)} %collective-permute-done.1, bf16[6,4,16,128]{3,0,2,1:T(8,128)(2,1)S(1)} %slice.1746, bf16[6,2,16,128]{3,0,2,1:T(8,128)(2,1)S(1)} %collective-permute-done), kind=kOutput, calls=%fused_computation.569 | convolution fusion | flops 71368704 | bytes 25436160 | tf_op jit(solution)/shard_map/dot_general | solution.py:41
  80.9 10.2 %fusion.350 = f32[6,16,128,512]{3,2,1,0:T(8,128)} fusion(bf16[9,512,6]{1,2,0:T(8,128)(2,1)S(1)} %slice_bitcast_fusion.7, bf16[6,2,16,128]{3,0,2,1:T(8,128)(2,1)S(1)} %collective-permute-done.1, bf16[6,4,16,128]{3,0,2,1:T(8,128)(2,1)S(1)} %slice.1746, bf16[6,2,16,128]{3,0,2,1:T(8,128)(2,1)S(1)} %collective-permute-done), kind=kOutput, calls=%fused_computation.567 | convolution fusion | flops 71368704 | bytes 25436160 | tf_op jit(solution)/shard_map/dot_general | solution.py:41
  91.0 10.1 %fusion.348 = f32[6,16,128,512]{3,2,1,0:T(8,128)} fusion(bf16[9,512,6]{1,2,0:T(8,128)(2,1)S(1)} %slice_bitcast_fusion.7, bf16[6,2,16,128]{3,0,2,1:T(8,128)(2,1)S(1)} %collective-permute-done.1, bf16[6,4,16,128]{3,0,2,1:T(8,128)(2,1)S(1)} %slice.1746, bf16[6,2,16,128]{3,0,2,1:T(8,128)(2,1)S(1)} %collective-permute-done), kind=kOutput, calls=%fused_computation.563 | convolution fusion | flops 71368704 | bytes 25436160 | tf_op jit(solution)/shard_map/dot_general | solution.py:41
  101.1 10.1 %fusion.222 = f32[6,16,128,512]{3,2,1,0:T(8,128)} fusion(bf16[6,2,16,128]{3,0,2,1:T(8,128)(2,1)S(1)} %collective-permute-done.1, bf16[6,4,16,128]{3,0,2,1:T(8,128)(2,1)S(1)} %slice.1746, bf16[9,512,6]{1,2,0:T(8,128)(2,1)S(1)} %slice_bitcast_fusion.7), kind=kOutput, calls=%fused_computation.332 | convolution fusion | flops 75571200 | bytes 25370624 | tf_op jit(solution)/shard_map/dot_general | solution.py:41
  111.2 10.3 %fusion.218 = f32[6,16,128,512]{3,2,1,0:T(8,128)} fusion(bf16[6,4,16,128]{3,0,2,1:T(8,128)(2,1)S(1)} %slice.1746, bf16[6,2,16,128]{3,0,2,1:T(8,128)(2,1)S(1)} %collective-permute-done, bf16[9,512,6]{1,2,0:T(8,128)(2,1)S(1)} %slice_bitcast_fusion.7), kind=kOutput, calls=%fused_computation.328 | convolution fusion | flops 75571200 | bytes 25370624 | tf_op jit(solution)/shard_map/dot_general | solution.py:41
  121.6 65.0 %fusion.3 = bf16[512,6,16,128]{0,3,2,1:T(8,128)(2,1)} fusion(f32[512]{0:T(512)S(1)} %get-tuple-element.131, f32[6,16,128,512]{3,2,1,0:T(8,128)} %fusion.222, f32[6,16,128,512]{3,2,1,0:T(8,128)} %fusion.347, f32[6,16,128,512]{3,2,1,0:T(8,128)} %fusion.348, f32[6,16,128,512]{3,2,1,0:T(8,128)} %fusion.349, f32[6,16,128,512]{3,2,1,0:T(8,128)} %fusion.350, ...), kind=kOutput, calls=%fused_computation.9 | convolution fusion | flops 140574720 | bytes 214181888 | tf_op jit(solution)/shard_map/dot_general | solution.py:41
  186.6 12.0 %fusion.2 = bf16[512,6,16,128]{0,3,2,1:T(8,128)(2,1)S(1)} fusion(f32[6]{0:T(128)S(1)} %and_convert_fusion.1, f32[512]{0:T(512)S(1)} %get-tuple-element.130, bf16[512,6,16,128]{0,3,2,1:T(8,128)(2,1)} %fusion.3, bf16[2,512,512]{2,1,0:T(8,128)(2,1)S(1)} %convert.15), kind=kOutput, calls=%fused_computation.8 | convolution fusion | flops 6467616768 | bytes 25692672 | tf_op jit(solution)/shard_map/dot_general | solution.py:155
  221.1 5.8 collective-permute-start.2
  264.3 19.1 %fusion.21 = bf16[512,4,8,128]{0,3,2,1:T(8,128)(2,1)} fusion(f32[512]{0:T(512)S(1)} %copy-done.50, f32[4,8,128,512]{3,2,1,0:T(8,128)} %fusion.272, f32[4,8,128,512]{3,2,1,0:T(8,128)S(1)} %fusion.324, f32[4,8,128,512]{3,2,1,0:T(8,128)} %fusion.325, f32[4,8,128,512]{3,2,1,0:T(8,128)S(1)} %fusion.326, f32[4,8,128,512]{3,2,1,0:T(8,128)} %fusion.327, ...), kind=kOutput, calls=%fused_computation.45 | convolution fusion | flops 67551232 | bytes 71518208 | tf_op jit(solution)/shard_map/dot_general | solution.py:41
  283.4 4.8 fusion.20
  299.1 8.0 all-reduce.31
  307.2 22.3 %all-reduce.30 = (f32[]{:T(128)}, f32[]{:T(128)}) all-reduce(f32[]{:T(128)} %get-tuple-element.66, f32[]{:T(128)} %get-tuple-element.67), channel_id=1, replica_groups=mesh['batch'=8,'rows'=4] {'batch'}, use_global_device_ids=true, to_apply=%region_2.3 | all-reduce | flops 2 | bytes 16 | tf_op jit(solution)/shard_map/psum | solution.py:279
  389.0 21.4 %fusion.13 = bf16[512,4,8,128]{0,3,2,1:T(8,128)(2,1)} fusion(f32[4,8,128,512]{3,2,1,0:T(8,128)} %fusion.238, f32[4,8,128,512]{3,2,1,0:T(8,128)} %fusion.306, f32[4,8,128,512]{3,2,1,0:T(8,128)} %fusion.307, f32[4,8,128,512]{3,2,1,0:T(8,128)S(1)} %fusion.308, f32[4,8,128,512]{3,2,1,0:T(8,128)} %fusion.309, f32[4,8,128,512]{3,2,1,0:T(8,128)} %fusion.310, ...), kind=kOutput, calls=%fused_computation.27 | convolution fusion | flops 112033792 | bytes 75816960 | tf_op jit(solution)/shard_map/dot_general | solution.py:41
  416.9 6.1 fusion.12
  471.5 10.6 %fusion.318 = f32[6,16,128,512]{3,2,1,0:T(8,128)} fusion(bf16[9,512,12]{1,2,0:T(8,128)(2,1)S(1)} %copy-done.36, bf16[12,2,16,128]{3,0,2,1:T(8,128)(2,1)S(1)} %collective-permute-done.11, bf16[12,4,16,128]{3,0,2,1:T(8,128)(2,1)S(1)} %get-tuple-element.84, bf16[12,2,16,128]{3,0,2,1:T(8,128)(2,1)S(1)} %collective-permute-done.10), kind=kOutput, calls=%fused_computation.481 | convolution fusion | flops 152174592 | bytes 25706496 | tf_op jit(solution)/shard_map/dot_general | solution.py:41
  482.1 10.1 %fusion.321 = f32[6,16,128,512]{3,2,1,0:T(8,128)} fusion(bf16[9,512,12]{1,2,0:T(8,128)(2,1)S(1)} %copy-done.36, bf16[12,2,16,128]{3,0,2,1:T(8,128)(2,1)S(1)} %collective-permute-done.11, bf16[12,4,16,128]{3,0,2,1:T(8,128)(2,1)S(1)} %get-tuple-element.84, bf16[12,2,16,128]{3,0,2,1:T(8,128)(2,1)S(1)} %collective-permute-done.10), kind=kOutput, calls=%fused_computation.488 | convolution fusion | flops 142737408 | bytes 25706496 | tf_op jit(solution)/shard_map/dot_general | solution.py:41
  492.2 10.1 %fusion.320 = f32[6,16,128,512]{3,2,1,0:T(8,128)} fusion(bf16[9,512,12]{1,2,0:T(8,128)(2,1)S(1)} %copy-done.36, bf16[12,2,16,128]{3,0,2,1:T(8,128)(2,1)S(1)} %collective-permute-done.11, bf16[12,4,16,128]{3,0,2,1:T(8,128)(2,1)S(1)} %get-tuple-element.84, bf16[12,2,16,128]{3,0,2,1:T(8,128)(2,1)S(1)} %collective-permute-done.10), kind=kOutput, calls=%fused_computation.485 | convolution fusion | flops 142737408 | bytes 25706496 | tf_op jit(solution)/shard_map/dot_general | solution.py:41
  502.2 10.1 %fusion.319 = f32[6,16,128,512]{3,2,1,0:T(8,128)} fusion(bf16[9,512,12]{1,2,0:T(8,128)(2,1)S(1)} %copy-done.36, bf16[12,2,16,128]{3,0,2,1:T(8,128)(2,1)S(1)} %collective-permute-done.11, bf16[12,4,16,128]{3,0,2,1:T(8,128)(2,1)S(1)} %get-tuple-element.84, bf16[12,2,16,128]{3,0,2,1:T(8,128)(2,1)S(1)} %collective-permute-done.10), kind=kOutput, calls=%fused_computation.483 | convolution fusion | flops 142737408 | bytes 25706496 | tf_op jit(solution)/shard_map/dot_general | solution.py:41
  512.4 10.1 %fusion.317 = f32[6,16,128,512]{3,2,1,0:T(8,128)} fusion(bf16[9,512,12]{1,2,0:T(8,128)(2,1)S(1)} %copy-done.36, bf16[12,2,16,128]{3,0,2,1:T(8,128)(2,1)S(1)} %collective-permute-done.11, bf16[12,4,16,128]{3,0,2,1:T(8,128)(2,1)S(1)} %get-tuple-element.84, bf16[12,2,16,128]{3,0,2,1:T(8,128)(2,1)S(1)} %collective-permute-done.10), kind=kOutput, calls=%fused_computation.479 | convolution fusion | flops 142737408 | bytes 25706496 | tf_op jit(solution)/shard_map/dot_general | solution.py:41
  522.5 10.0 %fusion.316 = f32[6,16,128,512]{3,2,1,0:T(8,128)} fusion(bf16[9,512,12]{1,2,0:T(8,128)(2,1)S(1)} %copy-done.36, bf16[12,2,16,128]{3,0,2,1:T(8,128)(2,1)S(1)} %collective-permute-done.11, bf16[12,4,16,128]{3,0,2,1:T(8,128)(2,1)S(1)} %get-tuple-element.84, bf16[12,2,16,128]{3,0,2,1:T(8,128)(2,1)S(1)} %collective-permute-done.10), kind=kOutput, calls=%fused_computation.477 | convolution fusion | flops 142737408 | bytes 25706496 | tf_op jit(solution)/shard_map/dot_general | solution.py:41
  532.5 10.1 %fusion.186 = f32[6,16,128,512]{3,2,1,0:T(8,128)} fusion(bf16[12,2,16,128]{3,0,2,1:T(8,128)(2,1)S(1)} %collective-permute-done.11, bf16[12,4,16,128]{3,0,2,1:T(8,128)(2,1)S(1)} %get-tuple-element.84, bf16[9,512,12]{1,2,0:T(8,128)(2,1)S(1)} %copy-done.36), kind=kOutput, calls=%fused_computation.276 | convolution fusion | flops 151142400 | bytes 25575424 | tf_op jit(solution)/shard_map/dot_general | solution.py:41
  542.6 10.2 %fusion.182 = f32[6,16,128,512]{3,2,1,0:T(8,128)} fusion(bf16[12,4,16,128]{3,0,2,1:T(8,128)(2,1)S(1)} %get-tuple-element.84, bf16[12,2,16,128]{3,0,2,1:T(8,128)(2,1)S(1)} %collective-permute-done.10, bf16[9,512,12]{1,2,0:T(8,128)(2,1)S(1)} %copy-done.36), kind=kOutput, calls=%fused_computation.272 | convolution fusion | flops 151142400 | bytes 25575424 | tf_op jit(solution)/shard_map/dot_general | solution.py:41
  552.8 68.5 %fusion.1 = bf16[512,6,16,128]{0,3,2,1:T(8,128)(2,1)} fusion(f32[6,16,128,512]{3,2,1,0:T(8,128)} %fusion.186, f32[6,16,128,512]{3,2,1,0:T(8,128)} %fusion.316, f32[6,16,128,512]{3,2,1,0:T(8,128)} %fusion.317, f32[6,16,128,512]{3,2,1,0:T(8,128)} %fusion.318, f32[6,16,128,512]{3,2,1,0:T(8,128)} %fusion.319, f32[6,16,128,512]{3,2,1,0:T(8,128)} %fusion.320, ...), kind=kOutput, calls=%fused_computation.3 | convolution fusion | flops 211943424 | bytes 227033088 | tf_op jit(solution)/shard_map/dot_general | solution.py:41
  621.3 11.3 %fusion.40 = f32[1,512,512]{2,1,0:T(8,128)} fusion(bf16[512,6,16,128]{0,3,2,1:T(8,128)(2,1)} %fusion.1, bf16[512,6,16,128]{0,3,2,1:T(8,128)(2,1)} %fusion.3), kind=kOutput, calls=%fused_computation.65 | convolution fusion | flops 4294967296 | bytes 22020096 | tf_op jit(solution)/shard_map/dot_general | solution.py:187
  632.7 16.2 %fusion = bf16[512,6,16,128]{0,3,2,1:T(8,128)(2,1)} fusion(bf16[512,6,16,128]{0,3,2,1:T(8,128)(2,1)} %fusion.3, bf16[512,6,16,128]{0,3,2,1:T(8,128)(2,1)} %fusion.1, bf16[2,512,512]{2,1,0:T(8,128)(2,1)S(1)} %copy-done.28), kind=kOutput, calls=%fused_computation.1 | convolution fusion | flops 6461325312 | bytes 38273024 | tf_op jit(solution)/shard_map/dot_general | solution.py:193
  649.0 5.8 fusion.344
  654.7 5.8 fusion.343
  699.5 39.0 %all-reduce.28 = (f32[1744]{0:T(1024)S(1)}, f32[1216]{0:T(1024)S(1)}, f32[9,48,24]{1,2,0:T(8,128)S(1)}) all-reduce(f32[1744]{0:T(1024)S(1)} %copy-done.54, f32[1216]{0:T(1024)S(1)} %concatenate.123, f32[9,48,24]{1,2,0:T(8,128)} %fusion.151), channel_id=1, replica_groups=mesh['batch'=8,'rows'=4] {'batch','rows'}, use_global_device_ids=true, to_apply=%region_32.33 | all-reduce | flops 13328 | bytes 106624 | tf_op jit(solution)/shard_map/psum | solution.py:316
  739.8 89.8 %all-reduce.34.cloned.1.call-done = (f32[9,12,512]{2,1,0:T(8,128)}, f32[9,6,512]{2,1,0:T(8,128)}, f32[1,512,512]{2,1,0:T(8,128)}, f32[1,512,512]{2,1,0:T(8,128)}...) async-done(((f32[9,12,512]{2,1,0:T(8,128)}, f32[9,6,512]{2,1,0:T(8,128)}, f32[1,512,512]{2,1,0:T(8,128)}, f32[1,512,512]{2,1,0:T(8,128)}, f32[9,24,512]{2,1,0:T(8,128)}, ...) | async-done | bytes 3092496 | tf_op jit(solution)/shard_map/psum | solution.py:316
  (440 shorter events, 271.4 us)
Async XLA Ops:
  7.2 822.5 %all-reduce.34.cloned.1.call-start = ((), (), s32[]{:S(2)}) async-start(), calls=%async_computation | async-start | bytes 6553600 | tf_op jit(solution)/shard_map/psum | solution.py:316
  14.7 218.6 %copy-start.7 = (bf16[6,4,16,128]{3,0,2,1:T(8,128)(2,1)}, bf16[6,4,16,128]{3,0,2,1:T(8,128)(2,1)S(1)}, u32[]{:S(2)}) copy-start(bf16[6,4,16,128]{3,0,2,1:T(8,128)(2,1)S(1)} %slice.1746) | copy-start | bytes 294916
  14.7 25.5 %collective-permute-start = (bf16[6,2,16,128]{3,0,2,1:T(8,128)(2,1)S(1)}, bf16[6,2,16,128]{3,0,2,1:T(8,128)(2,1)S(1)}, u32[]{:S(2)}, u32[]{:S(2)}) collective-permute-start(bf16[6,2,16,128]{3,0,2,1:T(8,128)(2,1)S(1)} %get-tuple-element.110), channel_id=1, source_target_pairs={{0,1},{1,2},{2,3},{4,5},{5,6},{6,7},{8,9},{9,10},{10,11},{12,13},{... | collective-permute-start | bytes 147464 | tf_op jit(solution)/shard_map/ppermute | solution.py:27
  17.1 23.1 %collective-permute-start.1 = (bf16[6,2,16,128]{3,0,2,1:T(8,128)(2,1)S(1)}, bf16[6,2,16,128]{3,0,2,1:T(8,128)(2,1)S(1)}, u32[]{:S(2)}, u32[]{:S(2)}) collective-permute-start(bf16[6,2,16,128]{3,0,2,1:T(8,128)(2,1)S(1)} %get-tuple-element.111), channel_id=1, source_target_pairs={{1,0},{2,1},{3,2},{5,4},{6,5},{7,6},{9,8},{10,9},{11,10},{13,12},{... | collective-permute-start | bytes 147464 | tf_op jit(solution)/shard_map/ppermute | solution.py:28
  23.1 27.4 %copy-start.25 = (bf16[9,512,12]{1,2,0:T(8,128)(2,1)}, bf16[9,512,12]{1,2,0:T(8,128)(2,1)S(1)}, u32[]{:S(2)}) copy-start(bf16[9,512,12]{1,2,0:T(8,128)(2,1)S(1)} %slice_bitcast_fusion.6) | copy-start | bytes 331780
  27.1 23.5 %copy-start.38 = (bf16[9,48,24]{1,2,0:T(8,128)(2,1)}, bf16[9,48,24]{1,2,0:T(8,128)(2,1)S(1)}, u32[]{:S(2)}) copy-start(bf16[9,48,24]{1,2,0:T(8,128)(2,1)S(1)} %convert_element_type.182) | copy-start | bytes 62212
  37.0 149.6 %copy-start.27 = (bf16[2,512,512]{2,1,0:T(8,128)(2,1)}, bf16[2,512,512]{2,1,0:T(8,128)(2,1)S(1)}, u32[]{:S(2)}) copy-start(bf16[2,512,512]{2,1,0:T(8,128)(2,1)S(1)} %convert.15) | copy-start | bytes 3145732
  40.2 193.1 %copy-start.12 = (bf16[6,2,16,128]{3,0,2,1:T(8,128)(2,1)}, bf16[6,2,16,128]{3,0,2,1:T(8,128)(2,1)S(1)}, u32[]{:S(2)}) copy-start(bf16[6,2,16,128]{3,0,2,1:T(8,128)(2,1)S(1)} %collective-permute-done) | copy-start | bytes 147460
  40.2 193.1 %copy-start.10 = (bf16[6,2,16,128]{3,0,2,1:T(8,128)(2,1)}, bf16[6,2,16,128]{3,0,2,1:T(8,128)(2,1)S(1)}, u32[]{:S(2)}) copy-start(bf16[6,2,16,128]{3,0,2,1:T(8,128)(2,1)S(1)} %collective-permute-done.1) | copy-start | bytes 147460
  198.7 18.2 %copy-start = (bf16[512,6,16,128]{0,3,2,1:T(8,128)(2,1)}, bf16[512,6,16,128]{0,3,2,1:T(8,128)(2,1)S(1)}, u32[]{:S(2)}) copy-start(bf16[512,6,16,128]{0,3,2,1:T(8,128)(2,1)S(1)} %fusion.2) | copy-start | bytes 37748740
  216.8 16.3 %copy-start.39 = (bf16[9,48,24]{1,2,0:T(8,128)(2,1)S(1)}, bf16[9,48,24]{1,2,0:T(8,128)(2,1)}, u32[]{:S(2)}) copy-start(bf16[9,48,24]{1,2,0:T(8,128)(2,1)} %copy-done.38) | copy-start | bytes 62212
  216.8 17.3 %copy-start.41 = (s32[4,16,128]{2,1,0:T(8,128)S(1)}, s32[4,16,128]{2,1,0:T(8,128)}, u32[]{:S(2)}) copy-start(s32[4,16,128]{2,1,0:T(8,128)} %param.22) | copy-start | bytes 98308
  216.8 17.9 %copy-start.26 = (bf16[9,512,12]{1,2,0:T(8,128)(2,1)S(1)}, bf16[9,512,12]{1,2,0:T(8,128)(2,1)}, u32[]{:S(2)}) copy-start(bf16[9,512,12]{1,2,0:T(8,128)(2,1)} %copy-done.25) | copy-start | bytes 331780
  219.0 16.9 %copy-start.18 = (f32[12,4,16,128]{3,0,2,1:T(8,128)}, f32[12,4,16,128]{3,0,2,1:T(8,128)S(1)}, u32[]{:S(2)}) copy-start(f32[12,4,16,128]{3,0,2,1:T(8,128)S(1)} %fusion.44) | copy-start | bytes 1179652
  219.8 74.4 %collective-permute-start.3 = (bf16[24,2,8,128]{3,0,2,1:T(8,128)(2,1)S(1)}, bf16[24,2,8,128]{3,0,2,1:T(8,128)(2,1)S(1)}, u32[]{:S(2)}, u32[]{:S(2)}) collective-permute-start(bf16[24,2,8,128]{3,0,2,1:T(8,128)(2,1)S(1)} %copy.686), channel_id=1, source_target_pairs={{1,0},{2,1},{3,2},{5,4},{6,5},{7,6},{9,8},{10,9},{11,10},{13,12},{... | collective-permute-start | bytes 294920 | tf_op jit(solution)/shard_map/ppermute | solution.py:28
  221.1 73.1 %collective-permute-start.2 = (bf16[24,2,8,128]{3,0,2,1:T(8,128)(2,1)S(1)}, bf16[24,2,8,128]{3,0,2,1:T(8,128)(2,1)S(1)}, u32[]{:S(2)}, u32[]{:S(2)}) collective-permute-start(bf16[24,2,8,128]{3,0,2,1:T(8,128)(2,1)S(1)} %copy.686), channel_id=1, source_target_pairs={{0,1},{1,2},{2,3},{4,5},{5,6},{6,7},{8,9},{9,10},{10,11},{12,13},{... | collective-permute-start | bytes 294920 | tf_op jit(solution)/shard_map/ppermute | solution.py:27
  227.3 7.4 collective-permute-start.5
  228.6 6.1 collective-permute-start.4
  264.3 19.1 %copy-start.72 = (f32[512]{0:T(512)S(1)}, f32[512]{0:T(512)}, u32[]{:S(2)}) copy-start(f32[512]{0:T(512)} %get-tuple-element.129) | copy-start | bytes 6148
  264.3 19.1 %copy-start.75 = (f32[4]{0:T(128)S(1)}, f32[4]{0:T(128)}, u32[]{:S(2)}) copy-start(f32[4]{0:T(128)} %and_convert_fusion) | copy-start | bytes 52
  295.5 50.1 %copy-start.43 = (bf16[9,24,48]{2,1,0:T(8,128)(2,1)S(1)}, bf16[9,24,48]{2,1,0:T(8,128)(2,1)}, u32[]{:S(2)}) copy-start(bf16[9,24,48]{2,1,0:T(8,128)(2,1)} %reverse_bitcast_fusion.4) | copy-start | bytes 62212
  330.1 15.6 %copy-start.3 = (bf16[512,4,8,128]{0,3,2,1:T(8,128)(2,1)S(1)}, bf16[512,4,8,128]{0,3,2,1:T(8,128)(2,1)}, u32[]{:S(2)}) copy-start(bf16[512,4,8,128]{0,3,2,1:T(8,128)(2,1)} %copy-done.2) | copy-start | bytes 12582916
  330.5 25.4 %collective-permute-start.7 = (bf16[24,2,8,128]{3,0,2,1:T(8,128)(2,1)S(1)}, bf16[24,2,8,128]{3,0,2,1:T(8,128)(2,1)S(1)}, u32[]{:S(2)}, u32[]{:S(2)}) collective-permute-start(bf16[24,2,8,128]{3,0,2,1:T(8,128)(2,1)S(1)} %get-tuple-element.92), channel_id=1, source_target_pairs={{1,0},{2,1},{3,2},{5,4},{6,5},{7,6},{9,8},{10,9},{11,10},{13,12},{... | collective-permute-start | bytes 294920 | tf_op jit(solution)/shard_map/ppermute | solution.py:28
  332.1 23.9 %collective-permute-start.6 = (bf16[24,2,8,128]{3,0,2,1:T(8,128)(2,1)S(1)}, bf16[24,2,8,128]{3,0,2,1:T(8,128)(2,1)S(1)}, u32[]{:S(2)}, u32[]{:S(2)}) collective-permute-start(bf16[24,2,8,128]{3,0,2,1:T(8,128)(2,1)S(1)} %get-tuple-element.92), channel_id=1, source_target_pairs={{0,1},{1,2},{2,3},{4,5},{5,6},{6,7},{8,9},{9,10},{10,11},{12,13},{... | collective-permute-start | bytes 294920 | tf_op jit(solution)/shard_map/ppermute | solution.py:27
  336.2 113.4 %collective-permute-start.9 = (bf16[48,2,8,128]{3,0,2,1:T(8,128)(2,1)S(1)}, bf16[48,2,8,128]{3,0,2,1:T(8,128)(2,1)S(1)}, u32[]{:S(2)}, u32[]{:S(2)}) collective-permute-start(bf16[48,2,8,128]{3,0,2,1:T(8,128)(2,1)S(1)} %get-tuple-element.86), channel_id=1, source_target_pairs={{1,0},{2,1},{3,2},{5,4},{6,5},{7,6},{9,8},{10,9},{11,10},{13,12},{... | collective-permute-start | bytes 589832 | tf_op jit(solution)/shard_map/ppermute | solution.py:28
  350.3 99.3 %collective-permute-start.8 = (bf16[48,2,8,128]{3,0,2,1:T(8,128)(2,1)S(1)}, bf16[48,2,8,128]{3,0,2,1:T(8,128)(2,1)S(1)}, u32[]{:S(2)}, u32[]{:S(2)}) collective-permute-start(bf16[48,2,8,128]{3,0,2,1:T(8,128)(2,1)S(1)} %get-tuple-element.86), channel_id=1, source_target_pairs={{0,1},{1,2},{2,3},{4,5},{5,6},{6,7},{8,9},{9,10},{10,11},{12,13},{... | collective-permute-start | bytes 589832 | tf_op jit(solution)/shard_map/ppermute | solution.py:27
  457.1 14.3 %collective-permute-start.10 = (bf16[12,2,16,128]{3,0,2,1:T(8,128)(2,1)S(1)}, bf16[12,2,16,128]{3,0,2,1:T(8,128)(2,1)S(1)}, u32[]{:S(2)}, u32[]{:S(2)}) collective-permute-start(bf16[12,2,16,128]{3,0,2,1:T(8,128)(2,1)S(1)} %get-tuple-element.105), channel_id=1, source_target_pairs={{0,1},{1,2},{2,3},{4,5},{5,6},{6,7},{8,9},{9,10},{10,11},{12,13},{... | collective-permute-start | bytes 294920 | tf_op jit(solution)/shard_map/ppermute | solution.py:27
  460.8 10.7 %collective-permute-start.11 = (bf16[12,2,16,128]{3,0,2,1:T(8,128)(2,1)S(1)}, bf16[12,2,16,128]{3,0,2,1:T(8,128)(2,1)S(1)}, u32[]{:S(2)}, u32[]{:S(2)}) collective-permute-start(bf16[12,2,16,128]{3,0,2,1:T(8,128)(2,1)S(1)} %get-tuple-element.106), channel_id=1, source_target_pairs={{1,0},{2,1},{3,2},{5,4},{6,5},{7,6},{9,8},{10,9},{11,10},{13,12},{... | collective-permute-start | bytes 294920 | tf_op jit(solution)/shard_map/ppermute | solution.py:28
  632.7 16.3 %copy-start.42 = (bf16[9,6,512]{2,1,0:T(8,128)(2,1)S(1)}, bf16[9,6,512]{2,1,0:T(8,128)(2,1)}, u32[]{:S(2)}) copy-start(bf16[9,6,512]{2,1,0:T(8,128)(2,1)} %reverse_bitcast_fusion.3) | copy-start | bytes 165892
  694.7 150.4 %copy-start.24 = (f32[9,18,512]{2,1,0:T(8,128)S(1)}, f32[9,18,512]{2,1,0:T(8,128)}, u32[]{:S(2)}) copy-start(f32[9,18,512]{2,1,0:T(8,128)} %param.26) | copy-start | bytes 995332
  694.7 152.9 %copy-start.21 = (f32[9,36,512]{2,1,0:T(8,128)S(1)}, f32[9,36,512]{2,1,0:T(8,128)}, u32[]{:S(2)}) copy-start(f32[9,36,512]{2,1,0:T(8,128)} %param.32) | copy-start | bytes 1990660
  829.6 15.5 %copy-start.35 = (f32[9,6,512]{2,1,0:T(8,128)S(1)}, f32[9,6,512]{2,1,0:T(8,128)}, u32[]{:S(2)}) copy-start(f32[9,6,512]{2,1,0:T(8,128)} %get-tuple-element.59) | copy-start | bytes 331780
  (60 other events, 330.5 us)
Sparse Core Ops, SparseCore 0:
  690.1 139.4 all-reduce.33
